TPU v7x, 512 devices: a whole 4x4x16 slice. The times are simulated.
512 devices in a mesh: grp: 32 (over x, y, z_hi), tile: 16 (over z_lo, core).
Axes of the slice: x: 4, y: 4, z: 16 (z_hi: 2, z_lo: 8; z = z_hi * 8 + z_lo), core: 2. Of those that a mesh axis runs over, the one named last changes fastest.
Arguments:
- log_cond: float32 [32, 128, 32, 128], P('grp', 'tile'), may hold values from -3 to 3
- potential: float32 [32, 128, 32, 128], P('grp', 'tile'), may hold values from -6 to 6
- noise: float32 [2, 32, 128, 32, 128], P(None, 'grp', 'tile'), may hold values from -3 to 3
- source: float32 [128, 32, 128], P('tile'), may hold values from -6 to 6
- parents: int32 [32], replicated, may hold values from 0 to 31
- accept: int32 [2, 32], P(None, 'grp'), may hold values 0 or 1
- weights: float32 [32], P('grp'), may hold values from 0.1 to 10
Outputs:
- conduct_out: float32 [32, 128, 32, 128], P('grp', 'tile')
- potential_out: float32 [32, 128, 32, 128], P('grp', 'tile')
- moments: float32 [1024, 1024], P('tile')
Inputs may be any that keep to these rules, and one draw needn't show every extreme that they name: `parents`: parent indices of offspring.
All inputs are finite; a program needn't handle non-finite values. No bound on the sum of `accept` on one device may be relied on, other than what follows from the above.
Results may differ from a plain program's by a relative error of at most 0.0001.
Values sent between devices are 32-bit elements; how exact they have to be, the bound alone decides.
A program may use at most 64 MiB of HBM per device.

v0:
```python
import jax
import jax.numpy as jnp
from jax import lax
from jax.sharding import PartitionSpec as P

prior_keep = 0.8
prior_fresh = 0.6
relax_weight = 0.8


def with_halo(block, sides, width):
    for axis, dim in sides:
        count = lax.axis_size(axis)
        forward = [(i, i + 1) for i in range(count - 1)]
        backward = [(target, source) for source, target in forward]
        low = lax.ppermute(
            lax.slice_in_dim(block, block.shape[dim] - width, None, axis=dim), axis, forward
        )
        high = lax.ppermute(lax.slice_in_dim(block, 0, width, axis=dim), axis, backward)
        block = jnp.concatenate([low, block, high], axis=dim)
    return block


def neighbours(padded):
    return [
        padded[2:, 1:-1, 1:-1],
        padded[:-2, 1:-1, 1:-1],
        padded[1:-1, 2:, 1:-1],
        padded[1:-1, :-2, 1:-1],
        padded[1:-1, 1:-1, 2:],
        padded[1:-1, 1:-1, :-2],
    ]


def relax_sweep(cond_ext, pot_ext, source):
    cond_pad = jnp.pad(cond_ext, ((0, 0), (1, 1), (1, 1)))
    pot_pad = jnp.pad(pot_ext, ((0, 0), (1, 1), (1, 1)))
    conductivity = jnp.exp(cond_pad)
    centre_k = conductivity[1:-1, 1:-1, 1:-1]
    centre = pot_pad[1:-1, 1:-1, 1:-1]
    flux_sum = jnp.zeros_like(centre)
    coef_sum = jnp.zeros_like(centre)
    for near_k, near_v in zip(neighbours(conductivity), neighbours(pot_pad)):
        face = 0.5 * (centre_k + near_k)
        flux_sum = flux_sum + face * near_v
        coef_sum = coef_sum + face
    return (1.0 - relax_weight) * centre + relax_weight * (source + flux_sum) / coef_sum


def local(log_cond, potential, noise, source, parents, accept, weights):
    mine = lax.axis_index("grp")
    bundle = jnp.stack([log_cond[0], potential[0]])
    parent = parents[mine]
    pieces = lax.all_gather(bundle[None], "grp", axis=0, tiled=True)
    owners = jnp.arange(pieces.shape[0], dtype=jnp.int32)
    chosen = jnp.where((owners == parent)[:, None, None, None, None], pieces, 0.0)
    moved = jnp.sum(chosen, axis=0)
    conduct = moved[0]
    pot = moved[1]
    width = conduct.shape[0]
    for move_index in range(noise.shape[0]):
        proposal = prior_keep * conduct + prior_fresh * noise[move_index, 0]
        extended = with_halo(jnp.stack([proposal, pot]), (("tile", 1),), 1)
        relaxed_once = relax_sweep(extended[0], extended[1], source)
        pot_ext = with_halo(relaxed_once, (("tile", 0),), 1)
        relaxed_twice = relax_sweep(extended[0], pot_ext, source)
        accepted = accept[move_index, 0] > 0
        conduct = jnp.where(accepted, proposal, conduct)
        pot = jnp.where(accepted, relaxed_twice, pot)
    weight_sum = lax.psum(jnp.sum(weights), "grp")
    share = weights[0] / weight_sum
    traces = jnp.transpose(pot, (1, 0, 2)).reshape(pot.shape[1], width * pot.shape[2])
    product = lax.dot_general(
        traces,
        traces,
        (((0,), (0,)), ((), ())),
        precision=lax.Precision.HIGHEST,
        preferred_element_type=jnp.float32,
    )
    partial_rows = lax.psum_scatter(share * product, "tile", scatter_dimension=0, tiled=True)
    moments = lax.psum(partial_rows, "grp")
    return (conduct[None], pot[None], moments)


def solution(mesh):
    placed = (
        P("grp", "tile", None, None),
        P("grp", "tile", None, None),
        P(None, "grp", "tile", None, None),
        P("tile", None, None),
        P(),
        P(None, "grp"),
        P("grp"),
    )
    return jax.shard_map(
        local,
        mesh=mesh,
        in_specs=placed,
        out_specs=(P("grp", "tile", None, None), P("grp", "tile", None, None), P("tile", None)),
        check_vma=False,
    )
```

profile of v0, /device:TPU:14, one launch (start us, length us, event | category | flops | bytes accessed | tf_op | source)
XLA Modules:
  0.0 1160.8 jit_solution(12140395760338257270)
XLA Ops:
  7.2 0.0 all-gather.3.cloned.1.call-start
  7.2 1.7 pad_maximum_fusion.2
  8.9 0.0 all-gather.3.cloned.1.call-update
  8.9 0.0 reduce-scatter.2.cloned.1.call-start
  9.0 1.3 fusion.101
  11.6 1.2 dynamic_slice.3
  12.8 0.6 iota_compare_fusion.4
  13.5 247.6 %all-gather.3.cloned.1.call-done = f32[64,8,32,128]{3,2,1,0:T(8,128)} async-done(((f32[2,8,32,128]{3,2,1,0:T(8,128)}), f32[64,8,32,128]{3,2,1,0:T(8,128)}) %all-gather.3.cloned.1.call-update) | async-done | bytes 8388624 | tf_op jit(solution)/shard_map/all_gather | solution.py:54
  261.1 0.0 copy-start.2
  261.1 0.0 copy-start
  261.1 4.6 select_reduce_fusion
  265.8 0.0 copy-done.2
  265.8 0.7 broadcast_select_fusion
  266.5 1.3 collective-permute-start
  267.8 1.3 collective-permute-start.1
  269.1 0.0 collective-permute-done
  269.1 1.8 collective-permute-done.1
  271.0 0.0 copy-done
  271.0 0.3 fusion.11
  271.3 1.3 collective-permute-start.2
  272.6 3.0 collective-permute-start.3
  275.6 0.0 collective-permute-done.2
  275.6 0.8 collective-permute-done.3
  276.4 0.2 select_maximum_fusion.2
  276.6 0.3 fusion.85
  276.9 7.9 collective-permute-start.4
  284.9 1.3 collective-permute-start.5
  286.2 0.0 collective-permute-done.4
  286.2 3.9 collective-permute-done.5
  290.1 0.3 fusion.23
  290.4 1.3 collective-permute-start.6
  291.7 6.7 collective-permute-start.7
  298.4 137.9 %psum.14 = f32[]{:T(128)} all-reduce(f32[]{:T(128)} %bitcast.17), channel_id=1, replica_groups=mesh['grp'=32,'tile'=16] {'grp'}, use_global_device_ids=true, to_apply=%region_1.2 | all-reduce | flops 1 | bytes 8 | tf_op jit(solution)/shard_map/psum | solution.py:70
  437.7 0.0 collective-permute-done.6
  437.7 0.0 collective-permute-done.7
  437.7 0.2 select_maximum_fusion
  437.9 0.3 fusion.66
  438.2 0.0 copy-start.1
  438.2 5.1 convolution_multiply_fusion
  443.3 0.0 reduce-scatter.2.cloned.1.call-update
  443.3 0.0 copy-done.1
  443.3 0.0 all-reduce.8.cloned.1.call-start
  443.3 130.4 %reduce-scatter.2.cloned.1.call-done = f32[64,1024]{1,0:T(8,128)} async-done(((f32[1024,1024]{1,0:T(8,128)}), f32[64,1024]{1,0:T(8,128)}) %reduce-scatter.2.cloned.1.call-update) | async-done | bytes 262160 | tf_op jit(solution)/shard_map/reduce_scatter | solution.py:80
  573.8 0.0 all-reduce.8.cloned.1.call-update
  573.8 578.8 %all-reduce.8.cloned.1.call-done = f32[64,1024]{1,0:T(8,128)} async-done(((f32[64,1024]{1,0:T(8,128)}), f32[64,1024]{1,0:T(8,128)}) %all-reduce.8.cloned.1.call-update) | async-done | bytes 262160 | tf_op jit(solution)/shard_map/psum | solution.py:81
  1152.6 1.7 copy.19
  (8 shorter events, 0.1 us)
Async XLA Ops:
  7.2 254.0 %all-gather.3.cloned.1.call-start = ((), (), s32[]{:S(2)}) async-start(), calls=%async_computation.3 | async-start | bytes 8650752 | tf_op jit(solution)/shard_map/all_gather | solution.py:54
  8.9 564.9 %reduce-scatter.2.cloned.1.call-start = ((), (), s32[]{:S(2)}) async-start(), calls=%async_computation.1 | async-start | bytes 4456448 | tf_op jit(solution)/shard_map/reduce_scatter | solution.py:80
  261.1 4.6 copy-start.2
  261.1 9.8 copy-start
  266.5 2.6 collective-permute-start
  267.8 3.1 collective-permute-start.1
  271.3 4.3 collective-permute-start.2
  272.6 3.9 collective-permute-start.3
  276.9 9.2 collective-permute-start.4
  284.9 5.2 collective-permute-start.5
  290.4 147.2 %collective-permute-start.6 = (f32[1,32,128]{2,1,0:T(8,128)S(1)}, f32[1,32,128]{2,1,0:T(8,128)S(1)}, u32[]{:S(2)}, u32[]{:S(2)}) collective-permute-start(f32[1,32,128]{2,1,0:T(8,128)S(1)} %get-tuple-element.16), channel_id=1, source_target_pairs={{1,0},{2,1},{3,2},{4,3},{5,4},{6,5},{7,6},{8,7},{9,8},{10,9},{11,1... | collective-permute-start | bytes 49160 | tf_op jit(solution)/shard_map/ppermute | solution.py:19
  291.7 146.0 %collective-permute-start.7 = (f32[1,32,128]{2,1,0:T(8,128)S(1)}, f32[1,32,128]{2,1,0:T(8,128)S(1)}, u32[]{:S(2)}, u32[]{:S(2)}) collective-permute-start(f32[1,32,128]{2,1,0:T(8,128)S(1)} %get-tuple-element.15), channel_id=1, source_target_pairs={{0,1},{1,2},{2,3},{3,4},{4,5},{5,6},{6,7},{7,8},{8,9},{9,10},{10,1... | collective-permute-start | bytes 49160 | tf_op jit(solution)/shard_map/ppermute | solution.py:16
  438.2 5.1 copy-start.1
  443.3 709.3 %all-reduce.8.cloned.1.call-start = ((), (), s32[]{:S(2)}) async-start(), calls=%async_computation.2 | async-start | bytes 524288 | tf_op jit(solution)/shard_map/psum | solution.py:81
Sparse Core Ops, SparseCore 0:
  12.9 248.2 all-gather.2
  443.4 130.3 reduce-scatter.1
  576.7 575.8 all-reduce.7
where the time goes:
time: 1160 us
  waiting for transfers between devices  963 us (83%)
  blocking collectives  138 us (12%)
  starting transfers between devices  24.2 us (2%)
  between operations  16.6 us (1%)
    psum x1, waiting for transfers between devices, local(): moments = lax.psum(partial_rows, 'grp')  579 us
    all_gather x1, waiting for transfers between devices, local(): pieces = lax.all_gather(bundle[None], 'grp', axis=0, tiled=True)  248 us
    psum x1, blocking collectives, local(): weight_sum = lax.psum(jnp.sum(weights), 'grp')  138 us
    reduce_scatter x1, waiting for transfers between devices, local(): lax.psum_scatter(share * product, 'tile', scatter_dimension=0, tiled=True)  130 us
  transfers between devices with their start and end apart: 11, of which 6 were waited for; matrix products, arithmetic and copies ran while one was open for 0% of the time, Pallas kernels for 0%

commit v1 on v0

--- a/solution.py
+++ b/solution.py
@@ -51,7 +51,9 @@
     mine = lax.axis_index("grp")
     bundle = jnp.stack([log_cond[0], potential[0]])
     parent = parents[mine]
-    pieces = lax.all_gather(bundle[None], "grp", axis=0, tiled=True)
+    pieces = jnp.concatenate(
+        lax.all_to_all(jnp.stack([bundle[None]] * lax.axis_size("grp")), "grp", 0, 0), axis=0
+    )
     owners = jnp.arange(pieces.shape[0], dtype=jnp.int32)
     chosen = jnp.where((owners == parent)[:, None, None, None, None], pieces, 0.0)
     moved = jnp.sum(chosen, axis=0)

time: 1160 us -> 1340 us (1.16)
  starting transfers between devices: 24.2 us -> 215 us
  waiting for transfers between devices: 963 us -> 942 us
    all_gather x1 -> x0, waiting for transfers between devices: 248 us -> none  [local(): pieces = lax.all_gather(bundle[None], 'grp', axis=0, tiled=True)]
    ppermute x4, starting transfers between devices: 18.9 us -> 189 us  [with_halo(): lax.ppermute(lax.slice_in_dim(block, block.shape[dim] - width, None, axis...]
    all_to_all x0 -> x1, waiting for transfers between devices: none -> 147 us  [local(): lax.all_to_all(jnp.stack([bundle[None]] * lax.axis_size('grp')), 'grp', 0...]
    ppermute x4, waiting for transfers between devices: 5.69 us -> 63.8 us  [with_halo(): lax.ppermute(lax.slice_in_dim(block, 0, width, axis=dim), axis, backward)]
    reduce_scatter x1, waiting for transfers between devices: 130 us -> 152 us  [local(): lax.psum_scatter(share * product, 'tile', scatter_dimension=0, tiled=True)]
    all_to_all x0 -> x1, starting transfers between devices: none -> 20.9 us  [local(): lax.all_to_all(jnp.stack([bundle[None]] * lax.axis_size('grp')), 'grp', 0...]
where the time goes in v1:
time: 1340 us
  waiting for transfers between devices  942 us (70%)
  starting transfers between devices  215 us (16%)
  blocking collectives  148 us (11%)
  between operations  16.9 us (1%)
    psum x1, waiting for transfers between devices, local(): moments = lax.psum(partial_rows, 'grp')  579 us
    ppermute x4, starting transfers between devices, with_halo(): lax.ppermute(lax.slice_in_dim(block, block.shape[dim] - width, None, axis...  189 us
    reduce_scatter x1, waiting for transfers between devices, local(): lax.psum_scatter(share * product, 'tile', scatter_dimension=0, tiled=True)  152 us
    psum x1, blocking collectives, local(): weight_sum = lax.psum(jnp.sum(weights), 'grp')  148 us
    all_to_all x1, waiting for transfers between devices, local(): lax.all_to_all(jnp.stack([bundle[None]] * lax.axis_size('grp')), 'grp', 0...  147 us
    ppermute x4, waiting for transfers between devices, with_halo(): lax.ppermute(lax.slice_in_dim(block, 0, width, axis=dim), axis, backward)  63.8 us
  transfers between devices with their start and end apart: 11, of which 6 were waited for; matrix products, arithmetic and copies ran while one was open for 0% of the time, Pallas kernels for 0%

profile of v1, /device:TPU:14, one launch (start us, length us, event | category | flops | bytes accessed | tf_op | source)
XLA Modules:
  0.0 1343.1 jit_solution(747564824424621438)
XLA Ops:
  7.2 1.0 pad_maximum_fusion.2
  8.2 4.3 stack.18
  12.5 20.9 %all-to-all-start = ((f32[32,1,2,8,32,128]{5,4,3,2,1,0:T(8,128)}), f32[32,1,2,8,32,128]{5,4,3,2,1,0:T(8,128)}, u32[]{:S(2)}, u32[]{:S(2)}) async-start(f32[32,1,2,8,32,128]{5,4,3,2,1,0:T(8,128)} %stack.18), calls=%async_computation | async-start | bytes 16777216 | tf_op jit(solution)/shard_map/all_to_all | solution.py:55
  33.4 0.0 copy-start.2
  33.4 0.0 copy-start
  33.5 0.0 reduce-scatter.2.cloned.1.call-start
  33.5 0.0 copy-done.3
  33.5 0.6 fusion.102
  35.4 0.0 copy-done.4
  35.4 0.6 dynamic_slice.3
  36.0 0.6 iota_compare_fusion.4
  36.7 146.8 %all-to-all-done = f32[32,1,2,8,32,128]{5,4,3,2,1,0:T(8,128)} async-done(((f32[32,1,2,8,32,128]{5,4,3,2,1,0:T(8,128)}), f32[32,1,2,8,32,128]{5,4,3,2,1,0:T(8,128)}, u32[]{:S(2)}, u32[]{:S(2)}) %all-to-all-start) | async-done | bytes 8388640 | tf_op jit(solution)/shard_map/all_to_all | solution.py:55
  183.5 4.6 fusion
  188.1 0.0 copy-done.2
  188.1 0.7 broadcast_select_fusion
  188.8 1.3 collective-permute-start
  190.1 1.3 collective-permute-start.1
  191.4 0.0 collective-permute-done
  191.4 31.6 %collective-permute-done.1 = f32[2,1,32,128]{3,2,1,0:T(8,128)S(1)} collective-permute-done((f32[2,1,32,128]{3,2,1,0:T(8,128)S(1)}, f32[2,1,32,128]{3,2,1,0:T(8,128)S(1)}, u32[]{:S(2)}, u32[]{:S(2)}) %collective-permute-start.1) | collective-permute-done | bytes 32800 | tf_op jit(solution)/shard_map/ppermute | solution.py:19
  223.1 0.0 copy-done
  223.1 0.3 fusion.12
  223.4 1.3 collective-permute-start.2
  224.7 68.3 %collective-permute-start.3 = (f32[1,32,128]{2,1,0:T(8,128)S(1)}, f32[1,32,128]{2,1,0:T(8,128)S(1)}, u32[]{:S(2)}, u32[]{:S(2)}) collective-permute-start(f32[1,32,128]{2,1,0:T(8,128)S(1)} %get-tuple-element.17), channel_id=1, source_target_pairs={{0,1},{1,2},{2,3},{3,4},{4,5},{5,6},{6,7},{7,8},{8,9},{9,10},{10,1... | collective-permute-start | bytes 49160 | tf_op jit(solution)/shard_map/ppermute | solution.py:16
  293.0 0.0 collective-permute-done.2
  293.0 0.8 collective-permute-done.3
  293.8 0.2 select_maximum_fusion.2
  294.0 0.3 fusion.86
  294.3 13.7 %collective-permute-start.4 = (f32[2,1,32,128]{3,2,1,0:T(8,128)S(1)}, f32[2,1,32,128]{3,2,1,0:T(8,128)S(1)}, u32[]{:S(2)}, u32[]{:S(2)}) collective-permute-start(f32[2,1,32,128]{3,2,1,0:T(8,128)S(1)} %get-tuple-element.10), channel_id=1, source_target_pairs={{0,1},{1,2},{2,3},{3,4},{4,5},{5,6},{6,7},{7,8},{8,9},{9,10},{10,1... | collective-permute-start | bytes 98312 | tf_op jit(solution)/shard_map/ppermute | solution.py:16
  308.0 1.3 collective-permute-start.5
  309.3 0.0 collective-permute-done.4
  309.3 32.2 %collective-permute-done.5 = f32[2,1,32,128]{3,2,1,0:T(8,128)S(1)} collective-permute-done((f32[2,1,32,128]{3,2,1,0:T(8,128)S(1)}, f32[2,1,32,128]{3,2,1,0:T(8,128)S(1)}, u32[]{:S(2)}, u32[]{:S(2)}) %collective-permute-start.5) | collective-permute-done | bytes 32800 | tf_op jit(solution)/shard_map/ppermute | solution.py:19
  341.6 0.3 fusion.24
  341.9 1.3 collective-permute-start.6
  343.2 105.9 %collective-permute-start.7 = (f32[1,32,128]{2,1,0:T(8,128)S(1)}, f32[1,32,128]{2,1,0:T(8,128)S(1)}, u32[]{:S(2)}, u32[]{:S(2)}) collective-permute-start(f32[1,32,128]{2,1,0:T(8,128)S(1)} %get-tuple-element.15), channel_id=1, source_target_pairs={{0,1},{1,2},{2,3},{3,4},{4,5},{5,6},{6,7},{7,8},{8,9},{9,10},{10,1... | collective-permute-start | bytes 49160 | tf_op jit(solution)/shard_map/ppermute | solution.py:16
  449.1 147.6 %psum.14 = f32[]{:T(128)} all-reduce(f32[]{:T(128)} %bitcast.17), channel_id=1, replica_groups=mesh['grp'=32,'tile'=16] {'grp'}, use_global_device_ids=true, to_apply=%region_1.2 | all-reduce | flops 1 | bytes 8 | tf_op jit(solution)/shard_map/psum | solution.py:72
  597.9 0.0 collective-permute-done.6
  597.9 0.0 collective-permute-done.7
  597.9 0.2 select_maximum_fusion
  598.1 0.3 fusion.67
  598.4 0.0 copy-start.1
  598.4 5.1 convolution_multiply_fusion
  603.6 0.0 reduce-scatter.2.cloned.1.call-update
  603.6 0.0 all-reduce.8.cloned.1.call-start
  603.6 152.2 %reduce-scatter.2.cloned.1.call-done = f32[64,1024]{1,0:T(8,128)} async-done(((f32[1024,1024]{1,0:T(8,128)}), f32[64,1024]{1,0:T(8,128)}) %reduce-scatter.2.cloned.1.call-update) | async-done | bytes 262160 | tf_op jit(solution)/shard_map/reduce_scatter | solution.py:82
  755.9 0.0 all-reduce.8.cloned.1.call-update
  755.9 578.8 %all-reduce.8.cloned.1.call-done = f32[64,1024]{1,0:T(8,128)} async-done(((f32[64,1024]{1,0:T(8,128)}), f32[64,1024]{1,0:T(8,128)}) %all-reduce.8.cloned.1.call-update) | async-done | bytes 262160 | tf_op jit(solution)/shard_map/psum | solution.py:83
  1334.6 1.7 copy.19
  1336.3 0.0 copy-done.1
  (10 shorter events, 0.1 us)
Async XLA Ops:
  12.5 21.0 %copy-start.3 = (s32[2,1]{0,1:T(1,128)S(1)}, s32[2,1]{0,1:T(1,128)}, u32[]{:S(2)}) copy-start(s32[2,1]{0,1:T(1,128)} %param.12) | copy-start | bytes 28
  12.5 22.9 %copy-start.4 = (s32[32]{0:T(128)S(1)}, s32[32]{0:T(128)}, u32[]{:S(2)}) copy-start(s32[32]{0:T(128)} %param.11) | copy-start | bytes 388
  12.5 171.0 %all-to-all-start = ((f32[32,1,2,8,32,128]{5,4,3,2,1,0:T(8,128)}), f32[32,1,2,8,32,128]{5,4,3,2,1,0:T(8,128)}, u32[]{:S(2)}, u32[]{:S(2)}) async-start(f32[32,1,2,8,32,128]{5,4,3,2,1,0:T(8,128)} %stack.18), calls=%async_computation | async-start | bytes 16777216 | tf_op jit(solution)/shard_map/all_to_all | solution.py:55
  33.4 154.6 %copy-start.2 = (f32[2,1,8,32,128]{4,3,2,1,0:T(8,128)S(1)}, f32[2,1,8,32,128]{4,3,2,1,0:T(8,128)}, u32[]{:S(2)}) copy-start(f32[2,1,8,32,128]{4,3,2,1,0:T(8,128)} %param.9) | copy-start | bytes 786436
  33.4 189.7 %copy-start = (f32[8,32,128]{2,1,0:T(8,128)S(1)}, f32[8,32,128]{2,1,0:T(8,128)}, u32[]{:S(2)}) copy-start(f32[8,32,128]{2,1,0:T(8,128)} %param.10) | copy-start | bytes 393220
  33.5 722.4 %reduce-scatter.2.cloned.1.call-start = ((), (), s32[]{:S(2)}) async-start(), calls=%async_computation.2 | async-start | bytes 4456448 | tf_op jit(solution)/shard_map/reduce_scatter | solution.py:82
  188.8 2.6 collective-permute-start
  190.1 33.0 %collective-permute-start.1 = (f32[2,1,32,128]{3,2,1,0:T(8,128)S(1)}, f32[2,1,32,128]{3,2,1,0:T(8,128)S(1)}, u32[]{:S(2)}, u32[]{:S(2)}) collective-permute-start(f32[2,1,32,128]{3,2,1,0:T(8,128)S(1)} %get-tuple-element.13), channel_id=1, source_target_pairs={{1,0},{2,1},{3,2},{4,3},{5,4},{6,5},{7,6},{8,7},{9,8},{10,9},{11,1... | collective-permute-start | bytes 98312 | tf_op jit(solution)/shard_map/ppermute | solution.py:19
  223.4 69.6 %collective-permute-start.2 = (f32[1,32,128]{2,1,0:T(8,128)S(1)}, f32[1,32,128]{2,1,0:T(8,128)S(1)}, u32[]{:S(2)}, u32[]{:S(2)}) collective-permute-start(f32[1,32,128]{2,1,0:T(8,128)S(1)} %get-tuple-element.18), channel_id=1, source_target_pairs={{1,0},{2,1},{3,2},{4,3},{5,4},{6,5},{7,6},{8,7},{9,8},{10,9},{11,1... | collective-permute-start | bytes 49160 | tf_op jit(solution)/shard_map/ppermute | solution.py:19
  224.7 69.1 %collective-permute-start.3 = (f32[1,32,128]{2,1,0:T(8,128)S(1)}, f32[1,32,128]{2,1,0:T(8,128)S(1)}, u32[]{:S(2)}, u32[]{:S(2)}) collective-permute-start(f32[1,32,128]{2,1,0:T(8,128)S(1)} %get-tuple-element.17), channel_id=1, source_target_pairs={{0,1},{1,2},{2,3},{3,4},{4,5},{5,6},{6,7},{7,8},{8,9},{9,10},{10,1... | collective-permute-start | bytes 49160 | tf_op jit(solution)/shard_map/ppermute | solution.py:16
  294.3 15.0 %collective-permute-start.4 = (f32[2,1,32,128]{3,2,1,0:T(8,128)S(1)}, f32[2,1,32,128]{3,2,1,0:T(8,128)S(1)}, u32[]{:S(2)}, u32[]{:S(2)}) collective-permute-start(f32[2,1,32,128]{3,2,1,0:T(8,128)S(1)} %get-tuple-element.10), channel_id=1, source_target_pairs={{0,1},{1,2},{2,3},{3,4},{4,5},{5,6},{6,7},{7,8},{8,9},{9,10},{10,1... | collective-permute-start | bytes 98312 | tf_op jit(solution)/shard_map/ppermute | solution.py:16
  308.0 33.5 %collective-permute-start.5 = (f32[2,1,32,128]{3,2,1,0:T(8,128)S(1)}, f32[2,1,32,128]{3,2,1,0:T(8,128)S(1)}, u32[]{:S(2)}, u32[]{:S(2)}) collective-permute-start(f32[2,1,32,128]{3,2,1,0:T(8,128)S(1)} %get-tuple-element.11), channel_id=1, source_target_pairs={{1,0},{2,1},{3,2},{4,3},{5,4},{6,5},{7,6},{8,7},{9,8},{10,9},{11,1... | collective-permute-start | bytes 98312 | tf_op jit(solution)/shard_map/ppermute | solution.py:19
  341.9 256.1 %collective-permute-start.6 = (f32[1,32,128]{2,1,0:T(8,128)S(1)}, f32[1,32,128]{2,1,0:T(8,128)S(1)}, u32[]{:S(2)}, u32[]{:S(2)}) collective-permute-start(f32[1,32,128]{2,1,0:T(8,128)S(1)} %get-tuple-element.16), channel_id=1, source_target_pairs={{1,0},{2,1},{3,2},{4,3},{5,4},{6,5},{7,6},{8,7},{9,8},{10,9},{11,1... | collective-permute-start | bytes 49160 | tf_op jit(solution)/shard_map/ppermute | solution.py:19
  343.2 254.8 %collective-permute-start.7 = (f32[1,32,128]{2,1,0:T(8,128)S(1)}, f32[1,32,128]{2,1,0:T(8,128)S(1)}, u32[]{:S(2)}, u32[]{:S(2)}) collective-permute-start(f32[1,32,128]{2,1,0:T(8,128)S(1)} %get-tuple-element.15), channel_id=1, source_target_pairs={{0,1},{1,2},{2,3},{3,4},{4,5},{5,6},{6,7},{7,8},{8,9},{9,10},{10,1... | collective-permute-start | bytes 49160 | tf_op jit(solution)/shard_map/ppermute | solution.py:16
  598.4 737.9 %copy-start.1 = (f32[8,32,128]{2,1,0:T(8,128)}, f32[8,32,128]{2,1,0:T(8,128)S(1)}, u32[]{:S(2)}) copy-start(f32[8,32,128]{2,1,0:T(8,128)S(1)} %fusion.67) | copy-start | bytes 393220
  603.6 731.1 %all-reduce.8.cloned.1.call-start = ((), (), s32[]{:S(2)}) async-start(), calls=%async_computation.3 | async-start | bytes 524288 | tf_op jit(solution)/shard_map/psum | solution.py:83
Sparse Core Ops, SparseCore 0:
  603.7 152.1 reduce-scatter.1
  758.8 575.8 all-reduce.7
